TPU v7x, 256 devices: a whole 4x4x8 slice. The times are simulated.
256 devices in a mesh: rows: 8 (over y, x_lo), cols: 32 (over z, x_hi, core).
Axes of the slice: x: 4 (x_hi: 2, x_lo: 2; x = x_hi * 2 + x_lo), y: 4, z: 8, core: 2. Of those that a mesh axis runs over, the one named last changes fastest.
Arguments:
- counts: bfloat16 [4096, 262144], P('rows', 'cols'), may hold values from 0 to 12, as said below
- start_a: float32 [4096, 128], P(('rows', 'cols')), may hold values from -0.4 to 0.4
- start_b: float32 [16384, 128], P(('cols', 'rows')), may hold values from -0.4 to 0.4
- start_c: float32 [16, 128], replicated, may hold values from -0.4 to 0.4
Outputs:
- factor_a: float32 [4096, 128], P(('rows', 'cols'))
- factor_b: float32 [16384, 128], P(('cols', 'rows'))
- factor_c: float32 [16, 128], replicated
Inputs may be any that keep to these rules, and one draw needn't show every extreme that they name: counts holds whole numbers.
All inputs are finite; a program needn't handle non-finite values.
Results may differ from a plain program's by a relative error of at most 0.009.
Values may be sent and summed in bfloat16 or wider, within the bound.
No kernel may reach another device: no remote copies, remote signals or barrier semaphores. Data moves between devices by JAX's collectives and lax.ppermute only.
A program may use at most 128 MiB of HBM per device.

v0:
```python
import math
import jax
import jax.numpy as jnp
from jax import lax
from jax.sharding import PartitionSpec as P

ITERS = 2


def local(counts, start_a, start_b, start_c):
    rows_here, flat_width = counts.shape
    depth = start_c.shape[0]
    cols_here = flat_width // depth
    total_i = rows_here * lax.axis_size("rows")
    total_j = cols_here * lax.axis_size("cols")
    rate_a = 0.3 / math.sqrt(total_j * depth)
    rate_b = 0.3 / math.sqrt(total_i * depth)
    rate_c = 0.3 / math.sqrt(total_i * total_j)
    local_a, local_b, shared_c = (start_a, start_b, start_c)
    for iteration in range(ITERS):
        low_a = lax.all_gather(local_a.astype(jnp.bfloat16), "cols", axis=0, tiled=True)
        low_b = lax.all_gather(local_b.astype(jnp.bfloat16), "rows", axis=0, tiled=True)
        low_b_wide = low_b.astype(jnp.float32)
        scaled = (low_b_wide[:, None, :] * shared_c[None, :, :]).astype(jnp.bfloat16)
        scaled = scaled.reshape(cols_here * depth, shared_c.shape[1])
        log_rate = lax.dot_general(
            low_a, scaled, (((1,), (1,)), ((), ())), preferred_element_type=jnp.float32
        )
        residual = (jnp.exp(log_rate) - counts.astype(jnp.float32)).astype(jnp.bfloat16)
        grad_a = jnp.dot(residual, scaled, preferred_element_type=jnp.float32)
        mixed = lax.dot_general(
            residual, low_a, (((0,), (0,)), ((), ())), preferred_element_type=jnp.float32
        )
        mixed = mixed.reshape(cols_here, depth, shared_c.shape[1])
        grad_b = jnp.sum(mixed * shared_c[None, :, :], axis=1)
        grad_c = jnp.sum(mixed * low_b_wide[:, None, :], axis=0)
        summed_a = lax.psum_scatter(grad_a, "cols", scatter_dimension=0, tiled=True)
        summed_b = lax.psum_scatter(grad_b, "rows", scatter_dimension=0, tiled=True)
        local_a = local_a - rate_a * summed_a
        local_b = local_b - rate_b * summed_b
        summed_c = lax.psum(grad_c, ("rows", "cols"))
        shared_c = shared_c - rate_c * summed_c
    return (local_a, local_b, shared_c)


def solution(mesh):
    placed = (P("rows", "cols"), P(("rows", "cols"), None), P(("cols", "rows"), None), P())
    return jax.shard_map(
        local,
        mesh=mesh,
        in_specs=placed,
        out_specs=(P(("rows", "cols"), None), P(("cols", "rows"), None), P()),
        check_vma=False,
    )
```

profile of v0, /device:TPU:32, one launch (start us, length us, event | category | flops | bytes accessed | tf_op | source)
XLA Modules:
  0.0 455.2 jit_solution(1326504930640590621)
XLA Ops:
  7.2 12.0 %copy.7 = bf16[512,8192]{0,1:T(8,128)(2,1)} copy(bf16[512,8192]{1,0:T(8,128)(2,1)} %param.4) | data formatting | bytes 16777216 | tf_op args[0]
  19.2 28.6 %all_gather.12 = bf16[512,128]{1,0:T(8,128)(2,1)S(1)} all-gather(bf16[64,128]{1,0:T(8,128)(2,1)S(1)} %convert_element_type.42), channel_id=1, replica_groups=mesh['rows'=8,'cols'=32] {'rows'}, dimensions={0}, use_global_device_ids=true | all-gather | bytes 147456 | tf_op jit(solution)/shard_map/all_gather | solution.py:22
  47.9 42.5 %all_gather.13 = bf16[512,128]{1,0:T(8,128)(2,1)S(1)} all-gather(bf16[16,128]{1,0:T(8,128)(2,1)S(1)} %convert_element_type.46), channel_id=1, replica_groups=mesh['rows'=8,'cols'=32] {'cols'}, dimensions={0}, use_global_device_ids=true | all-gather | bytes 135168 | tf_op jit(solution)/shard_map/all_gather | solution.py:21
  90.8 5.0 %fusion = bf16[512,8192]{0,1:T(8,128)(2,1)S(1)} fusion(bf16[512,8192]{0,1:T(8,128)(2,1)} %copy.7, bf16[8192,128]{1,0:T(8,128)(2,1)S(1)} %bitcast.22, bf16[512,128]{1,0:T(8,128)(2,1)S(1)} %all_gather.13), kind=kOutput, calls=%fused_computation.2 | convolution fusion | flops 1086324736 | bytes 19005440 | tf_op jit(solution)/shard_map/dot_general | solution.py:26
  95.8 3.2 copy-done
  99.0 3.0 fusion.4
  102.1 8.4 %multiply_reduce_fusion.3 = (f32[512,128]{1,0:T(8,128)}, f32[8192,128]{1,0:T(8,128)}) fusion(f32[16,128]{1,0:T(8,128)S(1)} %copy-done.5, bf16[512,8192]{0,1:T(8,128)(2,1)} %copy-done, bf16[512,128]{1,0:T(8,128)(2,1)S(1)} %all_gather.13), kind=kOutput, calls=%fused_computation.8 | convolution fusion | flops 1075773440 | bytes 12984320 | tf_op jit(solution)/shard_map/dot_general | solution.py:31
  110.6 2.8 multiply_reduce_fusion.2
  113.4 77.1 %psum.14 = f32[16,128]{1,0:T(8,128)S(1)} all-reduce(f32[16,128]{1,0:T(8,128)S(1)} %multiply_reduce_fusion.2), channel_id=1, replica_groups=mesh['rows'=8,'cols'=32] {'rows','cols'}, use_global_device_ids=true, to_apply=%region_4.0 | all-reduce | flops 2048 | bytes 16384 | tf_op jit(solution)/shard_map/psum | solution.py:41
  190.5 21.8 %reduce-scatter.5.cloned.1.call-done = f32[16,128]{1,0:T(8,128)} async-done(((f32[512,128]{1,0:T(8,128)}), f32[16,128]{1,0:T(8,128)}) %reduce-scatter.5.cloned.1.call-update) | async-done | bytes 8208 | tf_op jit(solution)/shard_map/reduce_scatter | solution.py:37
  213.0 38.0 %all_gather.14 = bf16[512,128]{1,0:T(8,128)(2,1)S(1)} all-gather(bf16[16,128]{1,0:T(8,128)(2,1)S(1)} %fusion.3), channel_id=1, replica_groups=mesh['rows'=8,'cols'=32] {'cols'}, dimensions={0}, use_global_device_ids=true | all-gather | bytes 135168 | tf_op jit(solution)/shard_map/all_gather | solution.py:21
  251.0 2.8 reduce-scatter.7.cloned.1.call-done
  253.8 0.8 fusion.2
  254.6 28.5 %all_gather.15 = bf16[512,128]{1,0:T(8,128)(2,1)S(1)} all-gather(bf16[64,128]{1,0:T(8,128)(2,1)S(1)} %fusion.2), channel_id=1, replica_groups=mesh['rows'=8,'cols'=32] {'rows'}, dimensions={0}, use_global_device_ids=true | all-gather | bytes 147456 | tf_op jit(solution)/shard_map/all_gather | solution.py:22
  283.5 5.0 %fusion.1 = bf16[512,8192]{0,1:T(8,128)(2,1)S(1)} fusion(bf16[512,8192]{0,1:T(8,128)(2,1)} %copy.7, bf16[512,128]{1,0:T(8,128)(2,1)S(1)} %all_gather.14, bf16[8192,128]{1,0:T(8,128)(2,1)S(1)} %bitcast.24), kind=kOutput, calls=%fused_computation.3 | convolution fusion | flops 1086324736 | bytes 19005440 | tf_op jit(solution)/shard_map/dot_general | solution.py:26
  288.5 3.2 copy-done.1
  291.7 3.1 fusion.5
  294.9 8.4 %multiply_reduce_fusion.1 = (f32[512,128]{1,0:T(8,128)}, f32[8192,128]{1,0:T(8,128)}) fusion(f32[16,128]{1,0:T(8,128)S(1)} %multiply_subtract_fusion.4, bf16[512,8192]{0,1:T(8,128)(2,1)} %copy-done.1, bf16[512,128]{1,0:T(8,128)(2,1)S(1)} %all_gather.14), kind=kOutput, calls=%fused_computation.5 | convolution fusion | flops 1075773440 | bytes 12984320 | tf_op jit(solution)/shard_map/dot_general | solution.py:31
  303.3 2.8 multiply_reduce_fusion
  306.1 73.2 %psum.15 = f32[16,128]{1,0:T(8,128)S(1)} all-reduce(f32[16,128]{1,0:T(8,128)S(1)} %multiply_reduce_fusion), channel_id=1, replica_groups=mesh['rows'=8,'cols'=32] {'rows','cols'}, use_global_device_ids=true, to_apply=%region_9.0 | all-reduce | flops 2048 | bytes 16384 | tf_op jit(solution)/shard_map/psum | solution.py:41
  380.0 25.9 %reduce-scatter.9.cloned.1.call-done = f32[16,128]{1,0:T(8,128)} async-done(((f32[512,128]{1,0:T(8,128)}), f32[16,128]{1,0:T(8,128)}) %reduce-scatter.9.cloned.1.call-update) | async-done | bytes 8208 | tf_op jit(solution)/shard_map/reduce_scatter | solution.py:37
  405.9 1.3 multiply_subtract_fusion.3
  407.2 40.1 %reduce-scatter.11.cloned.1.call-done = f32[64,128]{1,0:T(8,128)} async-done(((f32[512,128]{1,0:T(8,128)}), f32[64,128]{1,0:T(8,128)}) %reduce-scatter.11.cloned.1.call-update) | async-done | bytes 32784 | tf_op jit(solution)/shard_map/reduce_scatter | solution.py:38
  447.3 1.4 multiply_subtract_fusion
  (29 shorter events, 2.3 us)
Async XLA Ops:
  7.2 12.0 %copy-start.2 = (f32[64,128]{1,0:T(8,128)S(1)}, f32[64,128]{1,0:T(8,128)}, u32[]{:S(2)}) copy-start(f32[64,128]{1,0:T(8,128)} %param.6) | copy-start | bytes 98308
  7.2 40.7 %copy-start.4 = (f32[16,128]{1,0:T(8,128)S(1)}, f32[16,128]{1,0:T(8,128)}, u32[]{:S(2)}) copy-start(f32[16,128]{1,0:T(8,128)} %param.5) | copy-start | bytes 24580
  7.2 83.2 %copy-start.5 = (f32[16,128]{1,0:T(8,128)S(1)}, f32[16,128]{1,0:T(8,128)}, u32[]{:S(2)}) copy-start(f32[16,128]{1,0:T(8,128)} %param.7) | copy-start | bytes 24580
  7.2 205.1 %reduce-scatter.5.cloned.1.call-start = ((), (), s32[]{:S(2)}) async-start(), calls=%async_computation.4 | async-start | bytes 270336 | tf_op jit(solution)/shard_map/reduce_scatter | solution.py:37
  95.8 3.2 copy-start
  102.1 151.7 %reduce-scatter.7.cloned.1.call-start = ((), (), s32[]{:S(2)}) async-start(), calls=%async_computation.5 | async-start | bytes 294912 | tf_op jit(solution)/shard_map/reduce_scatter | solution.py:38
  110.5 295.3 %reduce-scatter.9.cloned.1.call-start = ((), (), s32[]{:S(2)}) async-start(), calls=%async_computation.6 | async-start | bytes 270336 | tf_op jit(solution)/shard_map/reduce_scatter | solution.py:37
  288.5 3.2 copy-start.1
  294.8 152.5 %reduce-scatter.11.cloned.1.call-start = ((), (), s32[]{:S(2)}) async-start(), calls=%async_computation.7 | async-start | bytes 294912 | tf_op jit(solution)/shard_map/reduce_scatter | solution.py:38
  303.3 102.6 %copy-start.6 = (f32[16,128]{1,0:T(8,128)S(1)}, f32[16,128]{1,0:T(8,128)}, u32[]{:S(2)}) copy-start(f32[16,128]{1,0:T(8,128)} %reduce-scatter.5.cloned.1.call-done) | copy-start | bytes 24580
  303.3 144.0 %copy-start.3 = (f32[64,128]{1,0:T(8,128)S(1)}, f32[64,128]{1,0:T(8,128)}, u32[]{:S(2)}) copy-start(f32[64,128]{1,0:T(8,128)} %reduce-scatter.7.cloned.1.call-done) | copy-start | bytes 98308
Sparse Core Ops, SparseCore 0:
  102.2 110.0 reduce-scatter.4
  214.8 38.9 reduce-scatter.6
  294.9 110.8 reduce-scatter.8
  408.4 38.8 reduce-scatter.10
where the time goes:
time: 456 us; the launch traced here: 455 us
  blocking collectives  288 us (63%)
  waiting for transfers between devices  90.7 us (20%)
  matrix products  33 us (7%)
  local copies, waits for them, and re-layouts  18.4 us (4%)
  between operations  13.9 us (3%)
  other arithmetic  11.1 us (2%)
    psum x2, blocking collectives, local(): summed_c = lax.psum(grad_c, ('rows', 'cols'))  150 us
    all_gather x2, blocking collectives, local(): lax.all_gather(local_a.astype(jnp.bfloat16), 'cols', axis=0, tiled=True)  80.5 us
    all_gather x2, blocking collectives, local(): lax.all_gather(local_b.astype(jnp.bfloat16), 'rows', axis=0, tiled=True)  57.1 us
    reduce_scatter x2, waiting for transfers between devices, local(): summed_a = lax.psum_scatter(grad_a, 'cols', scatter_dimension=0, tiled=True)  47.7 us
    reduce_scatter x2, waiting for transfers between devices, local(): summed_b = lax.psum_scatter(grad_b, 'rows', scatter_dimension=0, tiled=True)  42.9 us
    unnamed x15, local copies, waits for them, and re-layouts  18.4 us
    dot_general x2, matrix products, local(): lax.dot_general(residual, low_a, (((0,), (0,)), ((), ())), preferred_elem...  16.8 us
    dot_general x2, matrix products, local(): lax.dot_general(low_a, scaled, (((1,), (1,)), ((), ())), preferred_elemen...  10.1 us
  transfers between devices with their start and end apart: 4, of which 4 were waited for; matrix products, arithmetic and copies ran while one was open for 5% of the time, Pallas kernels for 0%

commit v1 on v0

--- a/solution.py
+++ b/solution.py
@@ -38,7 +38,8 @@
         summed_b = lax.psum_scatter(grad_b, "rows", scatter_dimension=0, tiled=True)
         local_a = local_a - rate_a * summed_a
         local_b = local_b - rate_b * summed_b
-        summed_c = lax.psum(grad_c, ("rows", "cols"))
+        mid_arr = lax.all_gather(grad_c, ("rows", "cols"))
+        summed_c = jnp.sum(mid_arr, axis=0)
         shared_c = shared_c - rate_c * summed_c
     return (local_a, local_b, shared_c)
 

time: 456 us -> 966 us (2.12)
  waiting for transfers between devices: 90.7 us -> 744 us
  blocking collectives: 288 us -> 138 us
    all_gather x0 -> x2, waiting for transfers between devices: none -> 505 us  [local(): mid_arr = lax.all_gather(grad_c, ('rows', 'cols'))]
    psum x2 -> x0, blocking collectives: 150 us -> none  [local(): summed_c = lax.psum(grad_c, ('rows', 'cols'))]
    reduce_scatter x2, waiting for transfers between devices: 47.7 us -> 196 us  [local(): summed_a = lax.psum_scatter(grad_a, 'cols', scatter_dimension=0, tiled=True)]
  transfers between devices with their start and end apart: 4 -> 6, of which waited for: 4 -> 6; matrix products, arithmetic and copies ran while one was open for 5% -> 3% of each run, Pallas kernels for 0% -> 0%
where the time goes in v1:
time: 966 us; the launch traced here: 965 us
  waiting for transfers between devices  744 us (77%)
  blocking collectives  138 us (14%)
  matrix products  33 us (3%)
  local copies, waits for them, and re-layouts  18.4 us (2%)
  other arithmetic  16 us (2%)
  between operations  15.3 us (2%)
    all_gather x2, waiting for transfers between devices, local(): mid_arr = lax.all_gather(grad_c, ('rows', 'cols'))  505 us
    reduce_scatter x2, waiting for transfers between devices, local(): summed_a = lax.psum_scatter(grad_a, 'cols', scatter_dimension=0, tiled=True)  196 us
    all_gather x2, blocking collectives, local(): lax.all_gather(local_a.astype(jnp.bfloat16), 'cols', axis=0, tiled=True)  80.6 us
    all_gather x2, blocking collectives, local(): lax.all_gather(local_b.astype(jnp.bfloat16), 'rows', axis=0, tiled=True)  57.2 us
    reduce_scatter x2, waiting for transfers between devices, local(): summed_b = lax.psum_scatter(grad_b, 'rows', scatter_dimension=0, tiled=True)  42.7 us
  transfers between devices with their start and end apart: 6, of which 6 were waited for; matrix products, arithmetic and copies ran while one was open for 3% of the time, Pallas kernels for 0%

profile of v1, /device:TPU:32, one launch (start us, length us, event | category | flops | bytes accessed | tf_op | source)
XLA Modules:
  0.0 964.9 jit_solution(435622260674065794)
XLA Ops:
  8.1 12.0 %copy.9 = bf16[512,8192]{0,1:T(8,128)(2,1)} copy(bf16[512,8192]{1,0:T(8,128)(2,1)} %param.4) | data formatting | bytes 16777216 | tf_op args[0]
  20.0 28.6 %all_gather.24 = bf16[512,128]{1,0:T(8,128)(2,1)S(1)} all-gather(bf16[64,128]{1,0:T(8,128)(2,1)S(1)} %convert_element_type.42), channel_id=1, replica_groups=mesh['rows'=8,'cols'=32] {'rows'}, dimensions={0}, use_global_device_ids=true | all-gather | bytes 147456 | tf_op jit(solution)/shard_map/all_gather | solution.py:22
  48.7 42.5 %all_gather.25 = bf16[512,128]{1,0:T(8,128)(2,1)S(1)} all-gather(bf16[16,128]{1,0:T(8,128)(2,1)S(1)} %convert_element_type.46), channel_id=1, replica_groups=mesh['rows'=8,'cols'=32] {'cols'}, dimensions={0}, use_global_device_ids=true | all-gather | bytes 135168 | tf_op jit(solution)/shard_map/all_gather | solution.py:21
  91.6 5.0 fusion
  96.7 3.2 copy-done
  99.9 3.0 fusion.4
  103.0 8.4 multiply_reduce_fusion.3
  111.4 3.4 multiply_reduce_fusion.2
  114.9 98.4 %reduce-scatter.5.cloned.1.call-done = f32[16,128]{1,0:T(8,128)} async-done(((f32[512,128]{1,0:T(8,128)}), f32[16,128]{1,0:T(8,128)}) %reduce-scatter.5.cloned.1.call-update) | async-done | bytes 8208 | tf_op jit(solution)/shard_map/reduce_scatter | solution.py:37
  213.9 38.1 %all_gather.26 = bf16[512,128]{1,0:T(8,128)(2,1)S(1)} all-gather(bf16[16,128]{1,0:T(8,128)(2,1)S(1)} %fusion.3), channel_id=1, replica_groups=mesh['rows'=8,'cols'=32] {'cols'}, dimensions={0}, use_global_device_ids=true | all-gather | bytes 135168 | tf_op jit(solution)/shard_map/all_gather | solution.py:21
  252.0 2.7 reduce-scatter.7.cloned.1.call-done
  255.5 28.5 %all_gather.27 = bf16[512,128]{1,0:T(8,128)(2,1)S(1)} all-gather(bf16[64,128]{1,0:T(8,128)(2,1)S(1)} %fusion.2), channel_id=1, replica_groups=mesh['rows'=8,'cols'=32] {'rows'}, dimensions={0}, use_global_device_ids=true | all-gather | bytes 147456 | tf_op jit(solution)/shard_map/all_gather | solution.py:22
  284.1 238.4 %all-gather.5.cloned.1.call-done = f32[4096,128]{1,0:T(8,128)} async-done(((f32[16,128]{1,0:T(8,128)}), f32[4096,128]{1,0:T(8,128)}) %all-gather.5.cloned.1.call-update) | async-done | bytes 2097168 | tf_op jit(solution)/shard_map/all_gather | solution.py:41
  522.5 1.9 reduce_sum.56
  524.7 5.0 fusion.1
  529.8 3.2 copy-done.1
  533.0 3.1 fusion.5
  536.1 8.4 multiply_reduce_fusion.1
  544.6 3.4 multiply_reduce_fusion
  548.0 97.9 %reduce-scatter.9.cloned.1.call-done = f32[16,128]{1,0:T(8,128)} async-done(((f32[512,128]{1,0:T(8,128)}), f32[16,128]{1,0:T(8,128)}) %reduce-scatter.9.cloned.1.call-update) | async-done | bytes 8208 | tf_op jit(solution)/shard_map/reduce_scatter | solution.py:37
  647.3 40.0 %reduce-scatter.11.cloned.1.call-done = f32[64,128]{1,0:T(8,128)} async-done(((f32[512,128]{1,0:T(8,128)}), f32[64,128]{1,0:T(8,128)}) %reduce-scatter.11.cloned.1.call-update) | async-done | bytes 32784 | tf_op jit(solution)/shard_map/reduce_scatter | solution.py:38
  687.3 1.4 multiply_subtract_fusion
  688.6 266.7 %all-gather.7.cloned.1.call-done = f32[4096,128]{1,0:T(8,128)} async-done(((f32[16,128]{1,0:T(8,128)}), f32[4096,128]{1,0:T(8,128)}) %all-gather.7.cloned.1.call-update) | async-done | bytes 2097168 | tf_op jit(solution)/shard_map/all_gather | solution.py:41
  955.3 1.9 reduce_sum.59
  (35 shorter events, 4.5 us)
Async XLA Ops:
  8.0 12.0 %copy-start.2 = (f32[64,128]{1,0:T(8,128)S(1)}, f32[64,128]{1,0:T(8,128)}, u32[]{:S(2)}) copy-start(f32[64,128]{1,0:T(8,128)} %param.6) | copy-start | bytes 98308
  8.0 40.7 %copy-start.4 = (f32[16,128]{1,0:T(8,128)S(1)}, f32[16,128]{1,0:T(8,128)}, u32[]{:S(2)}) copy-start(f32[16,128]{1,0:T(8,128)} %param.5) | copy-start | bytes 24580
  8.0 83.2 %copy-start.5 = (f32[16,128]{1,0:T(8,128)S(1)}, f32[16,128]{1,0:T(8,128)}, u32[]{:S(2)}) copy-start(f32[16,128]{1,0:T(8,128)} %param.7) | copy-start | bytes 24580
  8.0 205.2 %reduce-scatter.5.cloned.1.call-start = ((), (), s32[]{:S(2)}) async-start(), calls=%async_computation.4 | async-start | bytes 270336 | tf_op jit(solution)/shard_map/reduce_scatter | solution.py:37
  96.6 3.2 copy-start
  102.9 151.8 %reduce-scatter.7.cloned.1.call-start = ((), (), s32[]{:S(2)}) async-start(), calls=%async_computation.5 | async-start | bytes 294912 | tf_op jit(solution)/shard_map/reduce_scatter | solution.py:38
  111.4 411.1 %all-gather.5.cloned.1.call-start = ((), (), s32[]{:S(2)}) async-start(), calls=%async_computation.8 | async-start | bytes 2105344 | tf_op jit(solution)/shard_map/all_gather | solution.py:41
  114.8 531.1 %reduce-scatter.9.cloned.1.call-start = ((), (), s32[]{:S(2)}) async-start(), calls=%async_computation.6 | async-start | bytes 270336 | tf_op jit(solution)/shard_map/reduce_scatter | solution.py:37
  529.8 3.2 copy-start.1
  536.1 151.2 %reduce-scatter.11.cloned.1.call-start = ((), (), s32[]{:S(2)}) async-start(), calls=%async_computation.7 | async-start | bytes 294912 | tf_op jit(solution)/shard_map/reduce_scatter | solution.py:38
  544.5 101.4 %copy-start.6 = (f32[16,128]{1,0:T(8,128)S(1)}, f32[16,128]{1,0:T(8,128)}, u32[]{:S(2)}) copy-start(f32[16,128]{1,0:T(8,128)} %reduce-scatter.5.cloned.1.call-done) | copy-start | bytes 24580
  544.6 142.7 %copy-start.3 = (f32[64,128]{1,0:T(8,128)S(1)}, f32[64,128]{1,0:T(8,128)}, u32[]{:S(2)}) copy-start(f32[64,128]{1,0:T(8,128)} %reduce-scatter.7.cloned.1.call-done) | copy-start | bytes 98308
  544.6 410.7 %all-gather.7.cloned.1.call-start = ((), (), s32[]{:S(2)}) async-start(), calls=%async_computation.9 | async-start | bytes 2105344 | tf_op jit(solution)/shard_map/all_gather | solution.py:41
Sparse Core Ops, SparseCore 0:
  103.0 110.1 reduce-scatter.4
  215.7 38.9 reduce-scatter.6
  536.2 109.7 reduce-scatter.8
  648.5 38.7 reduce-scatter.10
Sparse Core Ops, SparseCore 1:
  114.9 407.5 all-gather.4
  548.1 407.1 all-gather.6
